TPU v7x, 128 devices: a whole 4x4x4 slice. The times are simulated.
128 devices in a mesh: prow: 16 (over x, z_hi, core), pcol: 8 (over z_lo, y).
Axes of the slice: x: 4, y: 4, z: 4 (z_hi: 2, z_lo: 2; z = z_hi * 2 + z_lo), core: 2. Of those that a mesh axis runs over, the one named last changes fastest.
Arguments:
- inverse: bfloat16 [4, 8192, 8, 4096], P(None, 'prow', None, 'pcol'), may hold values from -6 to 6
- panel: bfloat16 [2, 4, 8192, 256], P(None, None, 'prow'), may hold values from -0.0625 to 0.0625
- structure: int32 [2, 16], replicated, may hold values from 0 to 63, as said below
- diag_inverse: float32 [2, 256, 256], replicated, may hold values from -6 to 6
Outputs:
- off_diag: bfloat16 [2, 4, 8192, 256], P(None, None, ('prow', 'pcol'))
- diag_block: float32 [2, 256, 256], replicated
Inputs may be any that keep to these rules, and one draw needn't show every extreme that they name: `structure`: each row lists 16 distinct block indices in increasing order, exactly one of them congruent to p modulo 16 for every p, and always includes the last ancestor block 63.
All inputs are finite; a program needn't handle non-finite values.
Results may differ from a plain program's by a relative error of at most 0.0022.
Values may be sent and summed in bfloat16 or wider, within the bound.
No kernel may reach another device: no remote copies, remote signals or barrier semaphores. Data moves between devices by JAX's collectives and lax.ppermute only.
A program may use at most 128 MiB of HBM per device.

v0:
```python
import jax
import jax.numpy as jnp
from jax import lax
from jax.sharding import PartitionSpec as P


def cut_along(array, dim, count):
    before, after = (array.shape[:dim], array.shape[dim + 1 :])
    return jnp.moveaxis(array.reshape(*before, count, -1, *after), dim, 0)


def sum_at_owner(array, axis, dim):
    tiles = cut_along(array, dim, lax.axis_size(axis))
    arrived = lax.all_to_all(tiles, axis, split_axis=0, concat_axis=0, tiled=True)
    return arrived.sum(axis=0)


def on_device(inverse, panel, structure, diag_inverse):
    prow_count = lax.axis_size("prow")
    pcol_count = lax.axis_size("pcol")
    prow_index = lax.axis_index("prow")
    pcol_index = lax.axis_index("pcol")
    rows_local, block_size, cols_local, _ = inverse.shape
    panel_width = panel.shape[3]
    total_blocks = rows_local * prow_count
    piece_rows = block_size // pcol_count
    owner_ratio = prow_count // pcol_count
    repeat_count = cols_local // owner_ratio
    positions = jnp.arange(total_blocks, dtype=jnp.int32)
    local_rows = jnp.arange(rows_local, dtype=jnp.int32)
    pieces = []
    products = []
    for supernode in range(structure.shape[0]):
        chosen = structure[supernode]
        selected = jnp.any(chosen[:, None] == positions[None, :], axis=0)
        own_rows = lax.dynamic_index_in_dim(
            selected.reshape(rows_local, prow_count), prow_index, 1, keepdims=False
        )
        own_cols = lax.dynamic_index_in_dim(
            selected.reshape(cols_local, pcol_count), pcol_index, 1, keepdims=False
        )
        local_panel = panel[supernode]
        row_pick = jnp.sum(jnp.where(own_rows, local_rows, 0))
        single = lax.dynamic_index_in_dim(local_panel, row_pick, 0, keepdims=False)
        gathered = lax.all_gather(single, "prow", axis=0, tiled=True)
        gathered = gathered.reshape(owner_ratio, pcol_count, block_size, panel_width)
        owner_blocks = lax.dynamic_index_in_dim(gathered, pcol_index, 1, keepdims=False)
        tiled = jnp.broadcast_to(
            owner_blocks[None], (repeat_count, owner_ratio, block_size, panel_width)
        )
        tiled = tiled.reshape(cols_local, block_size, panel_width)
        column_panel = tiled * own_cols.astype(jnp.bfloat16)[:, None, None]
        ranking = jnp.where(own_cols, 0, cols_local) + jnp.arange(cols_local, dtype=jnp.int32)
        column_order = jnp.argsort(ranking)
        live_count = jnp.sum(own_cols.astype(jnp.int32))

        def add_column(position_index, running):
            column = column_order[position_index]
            block_column = lax.dynamic_index_in_dim(inverse, column, 2, keepdims=False)
            factor = lax.dynamic_index_in_dim(column_panel, column, 0, keepdims=False)
            return running + jnp.einsum(
                "rab,bw->raw", block_column, factor, preferred_element_type=jnp.float32
            )

        starting = jnp.zeros((rows_local, block_size, panel_width), jnp.float32)
        partial_value = lax.fori_loop(0, live_count, add_column, starting)
        partial_value = -partial_value * own_rows.astype(jnp.float32)[:, None, None]
        summed = sum_at_owner(partial_value, "pcol", 1)
        rounded = summed.astype(jnp.bfloat16)
        pieces.append(rounded)
        factor_rows = lax.dynamic_slice_in_dim(local_panel, pcol_index * piece_rows, piece_rows, 1)
        products.append(
            jnp.einsum("raw,rav->wv", factor_rows, rounded, preferred_element_type=jnp.float32)
        )
    diagonal_terms = lax.psum(jnp.stack(products), ("prow", "pcol"))
    return (jnp.stack(pieces), diag_inverse - diagonal_terms)


def solution(mesh):
    placed = (P(None, "prow", None, "pcol"), P(None, None, "prow", None), P(), P())
    return jax.shard_map(
        on_device,
        mesh=mesh,
        in_specs=placed,
        out_specs=(P(None, None, ("prow", "pcol"), None), P()),
        check_vma=False,
    )
```

profile of v0, /device:TPU:1, one launch (start us, length us, event | category | flops | bytes accessed | tf_op | source)
XLA Modules:
  0.0 347.8 jit_solution(9517647593599522379)
XLA Ops:
  7.2 0.8 slice_bitcast_fusion.1
  8.0 0.1 fusion.24
  8.3 0.2 fusion.28
  8.5 0.2 fusion.29
  8.7 0.6 select_reduce_fusion.2
  10.6 1.7 fusion.30
  13.0 0.7 constant_dynamic-slice_fusion.3
  15.7 0.7 constant_dynamic-slice_fusion
  16.7 16.7 %copy.16 = bf16[4,512,8,512]{3,1,0,2:T(8,128)(2,1)} copy(bf16[4,512,8,512]{3,2,1,0:T(8,128)(2,1)} %param.8) | data formatting | bytes 33554432 | tf_op jit(solution)/shard_map/while | solution.py:66
  33.3 0.2 convert_reduce_fusion.3
  33.5 0.8 select_reduce_fusion.1
  34.3 1.0 sort.31
  35.3 0.8 select_reduce_fusion
  36.1 37.5 %all-gather.5.cloned.1.call-done = bf16[1,1,8192,256]{3,2,1,0:T(8,128)(2,1)} async-done(((bf16[1,1,512,256]{3,2,1,0:T(8,128)(2,1)}), bf16[1,1,8192,256]{3,2,1,0:T(8,128)(2,1)}) %all-gather.5.cloned.1.call-update) | async-done | bytes 4194320 | tf_op jit(solution)/shard_map/all_gather | solution.py:45
  73.6 1.1 dynamic-slice_bitcast_fusion.1
  74.7 1.6 bitcast_multiply_fusion.1
  76.2 0.2 broadcast.9.clone.1
  76.4 11.7 %while.20 = (s32[]{:T(128)}, f32[4,512,256]{2,1,0:T(8,128)S(1)}, s32[]{:T(128)}, s32[8]{0:T(128)S(1)}, bf16[4,512,8,512]{3,1,0,2:T(8,128)(2,1)}, /*index=5*/bf16...) while((s32[]{:T(128)}, f32[4,512,256]{2,1,0:T(8,128)S(1)}, s32[]{:T(128)}, s32[8]{0:T(128)S(1)}, ...), condition=%wide.region_5.6_spmd, body=%wide.region_4.5_spmd.sunk | while | flops 537395200 | bytes 6554797 | solution.py:66
  77.1 0.6 dynamic_slice.130
  79.6 2.3 fusion.41
  82.5 0.6 dynamic_slice.130
  85.1 2.4 fusion.41
  88.1 0.3 negate_multiply_fusion.1
  88.4 1.5 copy.17
  89.9 4.3 %all-to-all-start = ((f32[8,4,64,256]{3,2,1,0:T(8,128)}), f32[8,4,64,256]{3,2,1,0:T(8,128)}, u32[]{:S(2)}, u32[]{:S(2)}) async-start(f32[8,4,64,256]{3,2,1,0:T(8,128)} %copy.17), calls=%async_computation | async-start | bytes 4194304 | tf_op jit(solution)/shard_map/all_to_all | solution.py:14
  94.2 0.2 convert_reduce_fusion.2
  94.4 1.0 sort.32
  95.5 45.2 %all-gather.7.cloned.1.call-done = bf16[1,1,8192,256]{3,2,1,0:T(8,128)(2,1)} async-done(((bf16[1,1,512,256]{3,2,1,0:T(8,128)(2,1)}), bf16[1,1,8192,256]{3,2,1,0:T(8,128)(2,1)}) %all-gather.7.cloned.1.call-update) | async-done | bytes 4194320 | tf_op jit(solution)/shard_map/all_gather | solution.py:45
  140.7 1.1 dynamic-slice_bitcast_fusion
  141.7 1.6 bitcast_multiply_fusion
  143.3 0.2 broadcast.9.clone
  143.5 11.8 %while.21 = (s32[]{:T(128)}, f32[4,512,256]{2,1,0:T(8,128)S(1)}, s32[]{:T(128)}, s32[8]{0:T(128)S(1)}, bf16[4,512,8,512]{3,1,0,2:T(8,128)(2,1)}, /*index=5*/bf16...) while((s32[]{:T(128)}, f32[4,512,256]{2,1,0:T(8,128)S(1)}, s32[]{:T(128)}, s32[8]{0:T(128)S(1)}, ...), condition=%wide.region_12.13_spmd, body=%wide.region_11.12_spmd.sunk | while | flops 537395200 | bytes 6554797 | solution.py:66
  144.2 0.6 dynamic_slice.133
  146.7 2.3 fusion.44
  149.8 0.6 dynamic_slice.133
  152.3 2.3 fusion.44
  155.3 0.3 negate_multiply_fusion
  155.6 1.5 copy.19
  157.1 4.3 %all-to-all-start.1 = ((f32[8,4,64,256]{3,2,1,0:T(8,128)}), f32[8,4,64,256]{3,2,1,0:T(8,128)S(1)}, u32[]{:S(2)}, u32[]{:S(2)}) async-start(f32[8,4,64,256]{3,2,1,0:T(8,128)} %copy.19), calls=%async_computation.1 | async-start | bytes 4194304 | tf_op jit(solution)/shard_map/all_to_all | solution.py:14
  161.4 1.7 reduce_sum.56
  163.1 1.8 convolution_bitcast_fusion.1
  165.0 23.5 %all-to-all-done.1 = f32[8,4,64,256]{3,2,1,0:T(8,128)S(1)} async-done(((f32[8,4,64,256]{3,2,1,0:T(8,128)}), f32[8,4,64,256]{3,2,1,0:T(8,128)S(1)}, u32[]{:S(2)}, u32[]{:S(2)}) %all-to-all-start.1) | async-done | bytes 2097184 | tf_op jit(solution)/shard_map/all_to_all | solution.py:14
  188.5 0.1 reduce_sum.59
  188.6 0.2 convolution_bitcast_fusion
  188.8 1.8 pad_maximum_fusion
  190.6 0.7 pad_maximum_fusion.1
  191.4 148.0 %all-reduce.2.cloned.1.call-done = f32[2,256,256]{2,1,0:T(8,128)} async-done(((f32[2,256,256]{2,1,0:T(8,128)}), f32[2,256,256]{2,1,0:T(8,128)}) %all-reduce.2.cloned.1.call-update) | async-done | bytes 524304 | tf_op jit(solution)/shard_map/psum | solution.py:75
  339.4 1.9 sub.3
  (22 shorter events, 0.6 us)
Async XLA Ops:
  7.2 66.4 %all-gather.5.cloned.1.call-start = ((), (), s32[]{:S(2)}) async-start(), calls=%async_computation.3 | async-start | bytes 4456448 | tf_op jit(solution)/shard_map/all_gather | solution.py:45
  12.3 21.0 %copy-start = (bf16[1,4,512,256]{3,2,1,0:T(8,128)(2,1)}, bf16[1,4,512,256]{3,2,1,0:T(8,128)(2,1)S(1)}, u32[]{:S(2)}) copy-start(bf16[1,4,512,256]{3,2,1,0:T(8,128)(2,1)S(1)} %get-tuple-element.162) | copy-start | bytes 3145732
  13.7 126.9 %all-gather.7.cloned.1.call-start = ((), (), s32[]{:S(2)}) async-start(), calls=%async_computation.4 | async-start | bytes 4456448 | tf_op jit(solution)/shard_map/all_gather | solution.py:45
  89.9 67.2 %all-to-all-start = ((f32[8,4,64,256]{3,2,1,0:T(8,128)}), f32[8,4,64,256]{3,2,1,0:T(8,128)}, u32[]{:S(2)}, u32[]{:S(2)}) async-start(f32[8,4,64,256]{3,2,1,0:T(8,128)} %copy.17), calls=%async_computation | async-start | bytes 4194304 | tf_op jit(solution)/shard_map/all_to_all | solution.py:14
  157.1 31.4 %all-to-all-start.1 = ((f32[8,4,64,256]{3,2,1,0:T(8,128)}), f32[8,4,64,256]{3,2,1,0:T(8,128)S(1)}, u32[]{:S(2)}, u32[]{:S(2)}) async-start(f32[8,4,64,256]{3,2,1,0:T(8,128)} %copy.19), calls=%async_computation.1 | async-start | bytes 4194304 | tf_op jit(solution)/shard_map/all_to_all | solution.py:14
  161.4 178.0 %all-reduce.2.cloned.1.call-start = ((), (), s32[]{:S(2)}) async-start(), calls=%async_computation.2 | async-start | bytes 1048576 | tf_op jit(solution)/shard_map/psum | solution.py:75
  188.6 150.8 %copy-start.1 = (f32[2,256,256]{2,1,0:T(8,128)S(1)}, f32[2,256,256]{2,1,0:T(8,128)}, u32[]{:S(2)}) copy-start(f32[2,256,256]{2,1,0:T(8,128)} %param.11) | copy-start | bytes 1572868
Sparse Core Ops, SparseCore 0:
  13.9 59.6 all-gather.4
  76.6 64.0 all-gather.6
  190.8 148.5 all-reduce.1
where the time goes:
time: 349 us; the launch traced here: 348 us
  waiting for transfers between devices  254 us (73%)
  local copies, waits for them, and re-layouts  29.1 us (8%)
  between operations  17.8 us (5%)
  other arithmetic  14.8 us (4%)
  loops' own time  11.8 us (3%)
  matrix products  11.4 us (3%)
  starting transfers between devices  8.73 us (3%)
    psum x1, waiting for transfers between devices, on_device(): diagonal_terms = lax.psum(jnp.stack(products), ('prow', 'pcol'))  148 us
    all_gather x2, waiting for transfers between devices, on_device(): gathered = lax.all_gather(single, 'prow', axis=0, tiled=True)  82.7 us
    all_to_all x2, waiting for transfers between devices, sum_at_owner(): lax.all_to_all(tiles, axis, split_axis=0, concat_axis=0, tiled=True)  23.5 us
    while x1, local copies, waits for them, and re-layouts, on_device(): partial_value = lax.fori_loop(0, live_count, add_column, starting)  16.7 us
    another operation x2, loops' own time, on_device(): partial_value = lax.fori_loop(0, live_count, add_column, starting)  11.8 us
    dot_general x4, matrix products, add_column(): jnp.einsum('rab,bw->raw', block_column, factor, preferred_element_type=jn...  9.32 us
    all_to_all x2, starting transfers between devices, sum_at_owner(): lax.all_to_all(tiles, axis, split_axis=0, concat_axis=0, tiled=True)  8.61 us
  transfers between devices with their start and end apart: 5, of which 4 were waited for; matrix products, arithmetic and copies ran while one was open for 13% of the time, Pallas kernels for 0%

commit v1 on v0

--- a/solution.py
+++ b/solution.py
@@ -2,6 +2,13 @@
 import jax.numpy as jnp
 from jax import lax
 from jax.sharding import PartitionSpec as P
+
+
+def gather_over(x, axis, d):
+    n_dev = lax.axis_size(axis)
+    blocks = jnp.stack([x for _ in range(n_dev)])
+    blocks = lax.all_to_all(blocks, axis, split_axis=0, concat_axis=0)
+    return jnp.concatenate(blocks, axis=d)
 
 
 def cut_along(array, dim, count):
@@ -42,7 +49,7 @@
         local_panel = panel[supernode]
         row_pick = jnp.sum(jnp.where(own_rows, local_rows, 0))
         single = lax.dynamic_index_in_dim(local_panel, row_pick, 0, keepdims=False)
-        gathered = lax.all_gather(single, "prow", axis=0, tiled=True)
+        gathered = gather_over(single, "prow", 0)
         gathered = gathered.reshape(owner_ratio, pcol_count, block_size, panel_width)
         owner_blocks = lax.dynamic_index_in_dim(gathered, pcol_index, 1, keepdims=False)
         tiled = jnp.broadcast_to(

time: 349 us -> 374 us (1.072)
  starting transfers between devices: 8.73 us -> 35 us
    all_gather x2 -> x0, waiting for transfers between devices: 82.7 us -> none  [on_device(): gathered = lax.all_gather(single, 'prow', axis=0, tiled=True)]
    all_to_all x0 -> x2, waiting for transfers between devices: none -> 68.4 us  [gather_over(): blocks = lax.all_to_all(blocks, axis, split_axis=0, concat_axis=0)]
    all_to_all x0 -> x2, starting transfers between devices: none -> 22.1 us  [gather_over(): blocks = lax.all_to_all(blocks, axis, split_axis=0, concat_axis=0)]
    all_to_all x2, waiting for transfers between devices: 23.5 us -> 33.8 us  [sum_at_owner(): lax.all_to_all(tiles, axis, split_axis=0, concat_axis=0, tiled=True)]
    another operation x2 -> x4, local copies, waits for them, and re-layouts: 0.31 us -> 5.02 us  [the longest x2 4.71 us: gather_over(): blocks = jnp.stack([x for _ in range(n_dev)])]
    all_to_all x2, starting transfers between devices: 8.61 us -> 12.9 us  [sum_at_owner(): lax.all_to_all(tiles, axis, split_axis=0, concat_axis=0, tiled=True)]
  transfers between devices with their start and end apart: 5 -> 5, of which waited for: 4 -> 5; matrix products, arithmetic and copies ran while one was open for 13% -> 12% of each run, Pallas kernels for 0% -> 0%
where the time goes in v1:
time: 374 us; the launch traced here: 373 us
  waiting for transfers between devices  252 us (67%)
  starting transfers between devices  35 us (9%)
  local copies, waits for them, and re-layouts  32.2 us (9%)
  between operations  18.1 us (5%)
  other arithmetic  14.6 us (4%)
  matrix products  11.3 us (3%)
  loops' own time  10.5 us (3%)
    psum x1, waiting for transfers between devices, on_device(): diagonal_terms = lax.psum(jnp.stack(products), ('prow', 'pcol'))  149 us
    all_to_all x2, waiting for transfers between devices, gather_over(): blocks = lax.all_to_all(blocks, axis, split_axis=0, concat_axis=0)  68.4 us
    all_to_all x2, waiting for transfers between devices, sum_at_owner(): lax.all_to_all(tiles, axis, split_axis=0, concat_axis=0, tiled=True)  33.8 us
    all_to_all x2, starting transfers between devices, gather_over(): blocks = lax.all_to_all(blocks, axis, split_axis=0, concat_axis=0)  22.1 us
    while x1, local copies, waits for them, and re-layouts, on_device(): partial_value = lax.fori_loop(0, live_count, add_column, starting)  16.6 us
    all_to_all x2, starting transfers between devices, sum_at_owner(): lax.all_to_all(tiles, axis, split_axis=0, concat_axis=0, tiled=True)  12.9 us
    another operation x2, loops' own time, on_device(): partial_value = lax.fori_loop(0, live_count, add_column, starting)  10.5 us
    dot_general x4, matrix products, add_column(): jnp.einsum('rab,bw->raw', block_column, factor, preferred_element_type=jn...  9.23 us
  transfers between devices with their start and end apart: 5, of which 5 were waited for; matrix products, arithmetic and copies ran while one was open for 12% of the time, Pallas kernels for 0%

profile of v1, /device:TPU:1, one launch (start us, length us, event | category | flops | bytes accessed | tf_op | source)
XLA Modules:
  0.0 373.4 jit_solution(6146794443949422200)
XLA Ops:
  7.2 0.8 slice_bitcast_fusion.1
  8.3 0.2 fusion.28
  8.5 0.2 fusion.29
  8.7 0.6 select_reduce_fusion.2
  10.6 1.7 fusion.30
  13.0 2.3 stack.12
  15.3 9.1 %all-to-all-start = ((bf16[16,512,256]{2,1,0:T(8,128)(2,1)}), bf16[16,512,256]{2,1,0:T(8,128)(2,1)}, u32[]{:S(2)}, u32[]{:S(2)}) async-start(bf16[16,512,256]{2,1,0:T(8,128)(2,1)} %stack.12), calls=%async_computation | async-start | bytes 8388608 | tf_op jit(solution)/shard_map/all_to_all | solution.py:10
  26.4 50.7 %all-to-all-done = bf16[16,512,256]{2,1,0:T(8,128)(2,1)} async-done(((bf16[16,512,256]{2,1,0:T(8,128)(2,1)}), bf16[16,512,256]{2,1,0:T(8,128)(2,1)}, u32[]{:S(2)}, u32[]{:S(2)}) %all-to-all-start) | async-done | bytes 4194336 | tf_op jit(solution)/shard_map/all_to_all | solution.py:10
  77.2 2.4 stack.13
  79.5 13.0 %all-to-all-start.2 = ((bf16[16,512,256]{2,1,0:T(8,128)(2,1)}), bf16[16,512,256]{2,1,0:T(8,128)(2,1)}, u32[]{:S(2)}, u32[]{:S(2)}) async-start(bf16[16,512,256]{2,1,0:T(8,128)(2,1)} %stack.13), calls=%async_computation.2 | async-start | bytes 8388608 | tf_op jit(solution)/shard_map/all_to_all | solution.py:10
  92.7 16.6 %copy.16 = bf16[4,512,8,512]{3,1,0,2:T(8,128)(2,1)} copy(bf16[4,512,8,512]{3,2,1,0:T(8,128)(2,1)} %param.8) | data formatting | bytes 33554432 | tf_op jit(solution)/shard_map/while | solution.py:73
  109.3 0.2 convert_reduce_fusion.3
  109.5 0.7 select_reduce_fusion.1
  110.2 1.0 sort.31
  111.2 0.7 select_reduce_fusion
  111.9 1.1 dynamic-slice_bitcast_fusion.1
  112.9 1.6 bitcast_multiply_fusion.1
  114.6 0.2 broadcast.11.clone.1
  114.7 11.0 %while.20 = (s32[]{:T(128)}, f32[4,512,256]{2,1,0:T(8,128)S(1)}, s32[]{:T(128)}, s32[8]{0:T(128)S(1)}, bf16[4,512,8,512]{3,1,0,2:T(8,128)(2,1)}, /*index=5*/bf16...) while((s32[]{:T(128)}, f32[4,512,256]{2,1,0:T(8,128)S(1)}, s32[]{:T(128)}, s32[8]{0:T(128)S(1)}, ...), condition=%wide.region_5.6_spmd, body=%wide.region_4.5_spmd.sunk | while | flops 537395200 | bytes 6554797 | solution.py:73
  115.4 0.6 dynamic_slice.136
  117.6 2.3 fusion.41
  120.6 0.6 dynamic_slice.136
  122.8 2.3 fusion.41
  125.7 0.3 negate_multiply_fusion.1
  126.0 1.5 copy.17
  127.5 17.7 %all-to-all-done.2 = bf16[16,512,256]{2,1,0:T(8,128)(2,1)} async-done(((bf16[16,512,256]{2,1,0:T(8,128)(2,1)}), bf16[16,512,256]{2,1,0:T(8,128)(2,1)}, u32[]{:S(2)}, u32[]{:S(2)}) %all-to-all-start.2) | async-done | bytes 4194336 | tf_op jit(solution)/shard_map/all_to_all | solution.py:10
  145.2 4.6 %all-to-all-start.1 = ((f32[8,4,64,256]{3,2,1,0:T(8,128)}), f32[8,4,64,256]{3,2,1,0:T(8,128)}, u32[]{:S(2)}, u32[]{:S(2)}) async-start(f32[8,4,64,256]{3,2,1,0:T(8,128)} %copy.17), calls=%async_computation.1 | async-start | bytes 4194304 | tf_op jit(solution)/shard_map/all_to_all | solution.py:21
  149.9 0.2 convert_reduce_fusion.2
  150.1 1.0 sort.32
  151.1 1.1 dynamic-slice_bitcast_fusion
  152.1 1.6 bitcast_multiply_fusion
  153.9 11.0 %while.21 = (s32[]{:T(128)}, f32[4,512,256]{2,1,0:T(8,128)S(1)}, s32[]{:T(128)}, s32[8]{0:T(128)S(1)}, bf16[4,512,8,512]{3,1,0,2:T(8,128)(2,1)}, /*index=5*/bf16...) while((s32[]{:T(128)}, f32[4,512,256]{2,1,0:T(8,128)S(1)}, s32[]{:T(128)}, s32[8]{0:T(128)S(1)}, ...), condition=%wide.region_12.13_spmd, body=%wide.region_11.12_spmd.sunk | while | flops 537395200 | bytes 6554797 | solution.py:73
  154.6 0.6 dynamic_slice.139
  156.8 2.3 fusion.44
  159.7 0.6 dynamic_slice.139
  161.9 2.3 fusion.44
  164.9 0.3 negate_multiply_fusion
  165.2 1.5 copy.19
  166.7 10.4 %all-to-all-done.1 = f32[8,4,64,256]{3,2,1,0:T(8,128)} async-done(((f32[8,4,64,256]{3,2,1,0:T(8,128)}), f32[8,4,64,256]{3,2,1,0:T(8,128)}, u32[]{:S(2)}, u32[]{:S(2)}) %all-to-all-start.1) | async-done | bytes 2097184 | tf_op jit(solution)/shard_map/all_to_all | solution.py:21
  177.1 8.2 %all-to-all-start.3 = ((f32[8,4,64,256]{3,2,1,0:T(8,128)}), f32[8,4,64,256]{3,2,1,0:T(8,128)S(1)}, u32[]{:S(2)}, u32[]{:S(2)}) async-start(f32[8,4,64,256]{3,2,1,0:T(8,128)} %copy.19), calls=%async_computation.3 | async-start | bytes 4194304 | tf_op jit(solution)/shard_map/all_to_all | solution.py:21
  185.4 1.7 reduce_sum.56
  187.1 1.8 convolution_bitcast_fusion.1
  189.0 23.4 %all-to-all-done.3 = f32[8,4,64,256]{3,2,1,0:T(8,128)S(1)} async-done(((f32[8,4,64,256]{3,2,1,0:T(8,128)}), f32[8,4,64,256]{3,2,1,0:T(8,128)S(1)}, u32[]{:S(2)}, u32[]{:S(2)}) %all-to-all-start.3) | async-done | bytes 2097184 | tf_op jit(solution)/shard_map/all_to_all | solution.py:21
  212.5 0.2 convolution_bitcast_fusion
  212.7 1.8 pad_maximum_fusion
  214.6 0.7 pad_maximum_fusion.1
  215.3 149.4 %all-reduce.2.cloned.1.call-done = f32[2,256,256]{2,1,0:T(8,128)} async-done(((f32[2,256,256]{2,1,0:T(8,128)}), f32[2,256,256]{2,1,0:T(8,128)}) %all-reduce.2.cloned.1.call-update) | async-done | bytes 524304 | tf_op jit(solution)/shard_map/psum | solution.py:82
  364.7 1.9 sub.3
  (22 shorter events, 0.9 us)
Async XLA Ops:
  12.3 3.0 copy-start
  15.3 61.9 %all-to-all-start = ((bf16[16,512,256]{2,1,0:T(8,128)(2,1)}), bf16[16,512,256]{2,1,0:T(8,128)(2,1)}, u32[]{:S(2)}, u32[]{:S(2)}) async-start(bf16[16,512,256]{2,1,0:T(8,128)(2,1)} %stack.12), calls=%async_computation | async-start | bytes 8388608 | tf_op jit(solution)/shard_map/all_to_all | solution.py:10
  79.5 65.7 %all-to-all-start.2 = ((bf16[16,512,256]{2,1,0:T(8,128)(2,1)}), bf16[16,512,256]{2,1,0:T(8,128)(2,1)}, u32[]{:S(2)}, u32[]{:S(2)}) async-start(bf16[16,512,256]{2,1,0:T(8,128)(2,1)} %stack.13), calls=%async_computation.2 | async-start | bytes 8388608 | tf_op jit(solution)/shard_map/all_to_all | solution.py:10
  145.2 31.9 %all-to-all-start.1 = ((f32[8,4,64,256]{3,2,1,0:T(8,128)}), f32[8,4,64,256]{3,2,1,0:T(8,128)}, u32[]{:S(2)}, u32[]{:S(2)}) async-start(f32[8,4,64,256]{3,2,1,0:T(8,128)} %copy.17), calls=%async_computation.1 | async-start | bytes 4194304 | tf_op jit(solution)/shard_map/all_to_all | solution.py:21
  177.1 35.2 %all-to-all-start.3 = ((f32[8,4,64,256]{3,2,1,0:T(8,128)}), f32[8,4,64,256]{3,2,1,0:T(8,128)S(1)}, u32[]{:S(2)}, u32[]{:S(2)}) async-start(f32[8,4,64,256]{3,2,1,0:T(8,128)} %copy.19), calls=%async_computation.3 | async-start | bytes 4194304 | tf_op jit(solution)/shard_map/all_to_all | solution.py:21
  185.3 179.3 %all-reduce.2.cloned.1.call-start = ((), (), s32[]{:S(2)}) async-start(), calls=%async_computation.4 | async-start | bytes 1048576 | tf_op jit(solution)/shard_map/psum | solution.py:82
  212.5 152.2 %copy-start.1 = (f32[2,256,256]{2,1,0:T(8,128)S(1)}, f32[2,256,256]{2,1,0:T(8,128)}, u32[]{:S(2)}) copy-start(f32[2,256,256]{2,1,0:T(8,128)} %param.11) | copy-start | bytes 1572868
Sparse Core Ops, SparseCore 0:
  214.7 149.9 all-reduce.1
